TPU v7x, 32 devices: a whole 2x2x4 slice. The times are simulated.
32 devices in a mesh: pairs: 2 (over y), ctx: 8 (over z, x), head: 2 (over core).
Axes of the slice: x: 2, y: 2, z: 4, core: 2. Of those that a mesh axis runs over, the one named last changes fastest.
Arguments:
- hidden: bfloat16 [16, 2, 8192], P(('pairs', 'ctx')), parts along dimension 0, may hold values from -6 to 6
- wq: bfloat16 [8192, 4096], P('ctx', 'head'), may hold values from -0.0625 to 0.0625
- wkv: bfloat16 [2, 8192, 512], P(None, 'ctx', 'head'), may hold values from -0.0625 to 0.0625
- bias_q: bfloat16 [4096], P('head'), may hold values from -5.2 to 5.2
- bias_kv: bfloat16 [2, 512], P(None, 'head'), may hold values from -5.2 to 5.2
- key_value_cache: bfloat16 [2, 8192, 512], P(None, ('pairs', 'ctx'), 'head'), parts along dimension 1, may hold values from -46 to 46, as said below
- prompt_len: int32 [2], P('pairs'), parts along dimension 0, may hold values from 512 to 4096
- resp_len: int32 [4], P('pairs'), parts along dimension 0, may hold values from 2 to 8
Outputs:
- attn_out: bfloat16 [16, 2, 4096], P(('pairs', 'ctx'), None, 'head'), parts along dimension 0
There are 2 independent parts, one for each index of `pairs`. A program takes and returns all parts, laid end to end along the dimension named above; an argument that names none is the same for every part. Nothing has to cross between parts.
Inputs may be any that keep to these rules, and one draw needn't show every extreme that they name: `key_value_cache`: entries beyond prompt_len are padding and must not be attended to. Prompt positions from prompt_len on are padding. Token slots of response r from resp_len[r] on are padding.
All inputs are finite; a program needn't handle non-finite values.
Results may differ from a plain program's by a relative error of at most 0.025.
Values may be sent and summed in bfloat16 or wider, within the bound.
No kernel may reach another device: no remote copies, remote signals or barrier semaphores. Data moves between devices by JAX's collectives and lax.ppermute only.
A program may use at most 64 MiB of HBM per device.

v0:
```python
import jax
import jax.numpy as jnp
from jax import lax
from jax.sharding import PartitionSpec as P

HEAD_SIZE = 128
NEG_FILL = -1e30


def shards(hidden, wq, wkv, bias_q, bias_kv, key_value_cache, prompt_len, resp_len):
    tok_dev = hidden.shape[0]
    ctx_index = lax.axis_index("ctx")
    resp_tokens = tok_dev * lax.axis_size("ctx")
    q_width = wq.shape[1]
    k_width = wkv.shape[2]
    kv_local = k_width // HEAD_SIZE
    query_group_width = q_width // k_width
    score_scale = HEAD_SIZE ** (-0.5)
    row_count = 2 * tok_dev
    columns = lax.all_to_all(hidden, "ctx", split_axis=2, concat_axis=0, tiled=True)
    flat_rows = columns.reshape(2 * resp_tokens, columns.shape[2])
    weights_all = jnp.concatenate((wq, wkv[0], wkv[1]), axis=1)
    bias_all = jnp.concatenate((bias_q, bias_kv[0], bias_kv[1])).astype(jnp.float32)
    summed = lax.psum(jnp.dot(flat_rows, weights_all, preferred_element_type=jnp.float32), "ctx")
    projected = (summed + bias_all).astype(jnp.bfloat16)
    owned = lax.dynamic_slice_in_dim(projected, ctx_index * row_count, row_count, 0)
    query_rows = projected[:, :q_width].reshape(
        2 * resp_tokens, kv_local, query_group_width, HEAD_SIZE
    )
    cache_len = key_value_cache.shape[1]
    key_block = min(512, cache_len)
    block_count = cache_len // key_block
    prompt_key_rows = key_value_cache[0].reshape(block_count, key_block, kv_local, HEAD_SIZE)
    prompt_value_rows = key_value_cache[1].reshape(block_count, key_block, kv_local, HEAD_SIZE)
    first_slot = ctx_index * cache_len
    live_limit = prompt_len[0]

    def visit(carry, inputs):
        running_max, running_sum, weighted = carry
        block_keys, block_values, block_index = inputs
        scores = (
            jnp.einsum("rgjd,kgd->grjk", query_rows, block_keys, preferred_element_type=jnp.float32)
            * score_scale
        )
        position = first_slot + block_index * key_block + lax.iota(jnp.int32, key_block)
        is_live = position < live_limit
        scores = jnp.where(is_live, scores, NEG_FILL)
        new_max = jnp.maximum(running_max, jnp.max(scores, axis=-1))
        unscaled = jnp.where(is_live, jnp.exp(scores - new_max[..., None]), 0.0)
        factor = jnp.exp(running_max - new_max)
        running_sum = running_sum * factor + jnp.sum(unscaled, axis=-1)
        weighted = weighted * factor[..., None] + jnp.einsum(
            "grjk,kgd->grjd",
            unscaled.astype(jnp.bfloat16),
            block_values,
            preferred_element_type=jnp.float32,
        )
        return ((new_max, running_sum, weighted), None)

    statistic_shape = (kv_local, 2 * resp_tokens, query_group_width)
    start_state = (
        jnp.full(statistic_shape, NEG_FILL, jnp.float32),
        jnp.zeros(statistic_shape, jnp.float32),
        jnp.zeros(statistic_shape + (HEAD_SIZE,), jnp.float32),
    )
    closing_state, unused = lax.scan(
        visit,
        start_state,
        (prompt_key_rows, prompt_value_rows, jnp.arange(block_count, dtype=jnp.int32)),
    )
    owned_q = owned[:, :q_width].reshape(tok_dev, 2, kv_local, query_group_width, HEAD_SIZE)
    fresh_key_rows = projected[:, q_width : q_width + k_width].reshape(
        resp_tokens, 2, kv_local, HEAD_SIZE
    )
    fresh_value_rows = projected[:, q_width + k_width :].reshape(
        resp_tokens, 2, kv_local, HEAD_SIZE
    )
    self_scores = (
        jnp.einsum("trgjd,urgd->gtrju", owned_q, fresh_key_rows, preferred_element_type=jnp.float32)
        * score_scale
    )
    token_pos = ctx_index * tok_dev + lax.iota(jnp.int32, tok_dev)
    key_pos = lax.iota(jnp.int32, resp_tokens)
    self_live = (key_pos[None, None, :] <= token_pos[:, None, None]) & (
        key_pos[None, None, :] < resp_len[None, :, None]
    )
    self_live = self_live[None, :, :, None, :]
    self_scores = jnp.where(self_live, self_scores, NEG_FILL)
    self_max = jnp.max(self_scores, axis=-1)
    self_weights = jnp.where(self_live, jnp.exp(self_scores - self_max[..., None]), 0.0)
    self_sum = jnp.sum(self_weights, axis=-1)
    self_acc = jnp.einsum(
        "gtrju,urgd->gtrjd",
        self_weights.astype(jnp.bfloat16),
        fresh_value_rows,
        preferred_element_type=jnp.float32,
    )
    lead_shape = (1, kv_local, resp_tokens, 2, query_group_width)
    remote_max, remote_sum, remote_acc = (
        lax.all_to_all(
            closing_state[0].reshape(lead_shape), "ctx", split_axis=2, concat_axis=0, tiled=True
        ),
        lax.all_to_all(
            closing_state[1].reshape(lead_shape), "ctx", split_axis=2, concat_axis=0, tiled=True
        ),
        lax.all_to_all(
            closing_state[2].reshape(lead_shape + (HEAD_SIZE,)),
            "ctx",
            split_axis=2,
            concat_axis=0,
            tiled=True,
        ),
    )
    overall = jnp.maximum(jnp.max(remote_max, axis=0), self_max)
    remote_factor = jnp.exp(remote_max - overall[None])
    prompt_acc = jnp.sum(remote_factor[..., None] * remote_acc, axis=0)
    prompt_total = jnp.sum(remote_factor * remote_sum, axis=0)
    self_factor = jnp.exp(self_max - overall)
    numerator = prompt_acc + self_factor[..., None] * self_acc
    denominator = prompt_total + self_factor * self_sum
    result = numerator / denominator[..., None]
    row_live = token_pos[:, None] < resp_len[None, :]
    result = jnp.where(row_live[None, :, :, None, None], result, 0.0)
    return jnp.transpose(result, (1, 2, 0, 3, 4)).reshape(tok_dev, 2, q_width).astype(jnp.bfloat16)


def solution(mesh):
    return jax.shard_map(
        shards,
        mesh=mesh,
        in_specs=(
            P(("pairs", "ctx"), None, None),
            P("ctx", "head"),
            P(None, "ctx", "head"),
            P("head"),
            P(None, "head"),
            P(None, ("pairs", "ctx"), "head"),
            P("pairs"),
            P("pairs"),
        ),
        out_specs=P(("pairs", "ctx"), None, "head"),
        check_vma=False,
    )
```

profile of v0, /device:TPU:0, one launch (start us, length us, event | category | flops | bytes accessed | tf_op | source)
XLA Modules:
  0.0 205.0 jit_solution(12979786244044143791)
XLA Ops:
  6.5 8.2 %copy.38 = bf16[1,2,8192]{1,0,2:T(2,128)(2,1)} copy(bf16[1,2,8192]{2,1,0:T(2,128)(2,1)} %param.8) | data formatting | bytes 65536 | tf_op args[0]
  14.8 0.5 broadcast.132
  15.3 45.3 %reduce.10 = bf16[8192,2]{1,0:T(8,128)(2,1)S(1)} reduce(bf16[8192,1,2]{2,1,0:T(2,128)(2,1)} %bitcast.123, bf16[]{:T(256)} %broadcast.132), dimensions={1}, to_apply=%bitcast.111.reduce_sub_computation | reduce | bytes 65538
  60.6 3.8 %reshape.289 = bf16[8,2,1024]{2,1,0:T(2,128)(2,1)} reshape(bf16[8192,2]{1,0:T(8,128)(2,1)S(1)} %reduce.10) | data formatting | bytes 65536
  64.4 7.3 %all-to-all-start = ((bf16[8,2,1024]{2,1,0:T(2,128)(2,1)}), bf16[8,2,1024]{2,1,0:T(2,128)(2,1)S(1)}, u32[]{:S(2)}, u32[]{:S(2)}) async-start(bf16[8,2,1024]{2,1,0:T(2,128)(2,1)} %reshape.289), calls=%async_computation | async-start | bytes 65536 | tf_op jit(solution)/shard_map/all_to_all | solution.py:20
  71.8 1.1 fusion.45
  73.7 4.7 %all-to-all-done = bf16[8,2,1024]{2,1,0:T(2,128)(2,1)S(1)} async-done(((bf16[8,2,1024]{2,1,0:T(2,128)(2,1)}), bf16[8,2,1024]{2,1,0:T(2,128)(2,1)S(1)}, u32[]{:S(2)}, u32[]{:S(2)}) %all-to-all-start) | async-done | bytes 32800 | tf_op jit(solution)/shard_map/all_to_all | solution.py:20
  78.4 6.3 %reshape.290 = bf16[8192,1,2]{2,1,0:T(2,128)(2,1)} reshape(bf16[8,2,1024]{2,1,0:T(2,128)(2,1)S(1)} %all-to-all-done) | data formatting | bytes 65536
  84.7 8.1 %copy.39 = bf16[1,2,8192]{2,1,0:T(2,128)(2,1)S(1)} copy(bf16[1,2,8192]{1,0,2:T(2,128)(2,1)} %bitcast.124) | data formatting | bytes 65536 | tf_op jit(solution)/shard_map/all_to_all | solution.py:20
  92.9 3.3 %fusion.6 = f32[16,2560]{1,0:T(8,128)} fusion(bf16[16,1024]{1,0:T(8,128)(2,1)S(1)} %reshape.278, bf16[1024,256]{1,0:T(8,128)(2,1)S(1)} %get-tuple-element.26, bf16[1024,256]{1,0:T(8,128)(2,1)S(1)} %get-tuple-element.25, bf16[1024,2048]{1,0:T(8,128)(2,1)} %param.9), kind=kOutput, calls=%fused_computation.6 | convolution fusion | flops 99614720 | bytes 5439488 | tf_op jit(solution)/shard_map/dot_general | solution.py:24
  96.6 67.2 %all-reduce.2.cloned.1.call-done = f32[16,2560]{1,0:T(8,128)} async-done(((f32[16,2560]{1,0:T(8,128)}), f32[16,2560]{1,0:T(8,128)}) %all-reduce.2.cloned.1.call-update) | async-done | bytes 163856 | tf_op jit(solution)/shard_map/psum | solution.py:24
  163.8 0.9 add_convert_fusion
  164.7 0.3 fusion.47
  165.1 0.6 copy.44
  165.7 4.4 %all-to-all-start.1 = ((f32[1,2,8,2,8]{4,3,1,0,2:T(2,128)}), f32[1,2,8,2,8]{4,3,1,0,2:T(2,128)S(1)}, u32[]{:S(2)}, u32[]{:S(2)}) async-start(f32[1,2,8,2,8]{4,3,1,0,2:T(2,128)} %copy.44), calls=%async_computation.1 | async-start | bytes 32768 | tf_op jit(solution)/shard_map/all_to_all | solution.py:100
  170.4 0.3 convolution_add_fusion
  170.9 0.6 copy.49
  171.5 0.6 copy.52
  172.1 4.5 %all-to-all-done.1 = f32[1,2,8,2,8]{4,3,1,0,2:T(2,128)S(1)} async-done(((f32[1,2,8,2,8]{4,3,1,0,2:T(2,128)}), f32[1,2,8,2,8]{4,3,1,0,2:T(2,128)S(1)}, u32[]{:S(2)}, u32[]{:S(2)}) %all-to-all-start.1) | async-done | bytes 1056 | tf_op jit(solution)/shard_map/all_to_all | solution.py:100
  176.6 3.3 %all-to-all-start.3 = ((f32[1,2,8,2,8]{4,3,1,0,2:T(2,128)}), f32[1,2,8,2,8]{4,3,1,0,2:T(2,128)S(1)}, u32[]{:S(2)}, u32[]{:S(2)}) async-start(f32[1,2,8,2,8]{4,3,1,0,2:T(2,128)} %copy.52), calls=%async_computation.3 | async-start | bytes 32768 | tf_op jit(solution)/shard_map/all_to_all | solution.py:103
  180.0 6.5 %all-to-all-done.3 = f32[1,2,8,2,8]{4,3,1,0,2:T(2,128)S(1)} async-done(((f32[1,2,8,2,8]{4,3,1,0,2:T(2,128)}), f32[1,2,8,2,8]{4,3,1,0,2:T(2,128)S(1)}, u32[]{:S(2)}, u32[]{:S(2)}) %all-to-all-start.3) | async-done | bytes 1056 | tf_op jit(solution)/shard_map/all_to_all | solution.py:103
  186.5 3.4 %all-to-all-start.2 = ((f32[1,2,8,2,8,128]{5,4,3,1,0,2:T(8,128)}), f32[1,2,8,2,8,128]{5,4,3,1,0,2:T(8,128)S(1)}, u32[]{:S(2)}, u32[]{:S(2)}) async-start(f32[1,2,8,2,8,128]{5,4,3,1,0,2:T(8,128)} %copy.49), calls=%async_computation.2 | async-start | bytes 262144 | tf_op jit(solution)/shard_map/all_to_all | solution.py:106
  190.0 7.2 %all-to-all-done.2 = f32[1,2,8,2,8,128]{5,4,3,1,0,2:T(8,128)S(1)} async-done(((f32[1,2,8,2,8,128]{5,4,3,1,0,2:T(8,128)}), f32[1,2,8,2,8,128]{5,4,3,1,0,2:T(8,128)S(1)}, u32[]{:S(2)}, u32[]{:S(2)}) %all-to-all-start.2) | async-done | bytes 131104 | tf_op jit(solution)/shard_map/all_to_all | solution.py:106
  197.5 0.6 convert_element_type.36
  (41 shorter events, 1.6 us)
Async XLA Ops:
  15.3 57.6 %copy-start = (bf16[2,1024,256]{2,1,0:T(8,128)(2,1)S(1)}, bf16[2,1024,256]{2,1,0:T(8,128)(2,1)}, u32[]{:S(2)}) copy-start(bf16[2,1024,256]{2,1,0:T(8,128)(2,1)} %param.10) | copy-start | bytes 3145732
  60.6 13.0 %copy-start.3 = (s32[2]{0:T(128)S(1)}, s32[2]{0:T(128)}, u32[]{:S(2)}) copy-start(s32[2]{0:T(128)} %param.15) | copy-start | bytes 28
  60.6 13.1 %copy-start.2 = (bf16[2,256]{1,0:T(2,128)(2,1)S(1)}, bf16[2,256]{1,0:T(2,128)(2,1)}, u32[]{:S(2)}) copy-start(bf16[2,256]{1,0:T(2,128)(2,1)} %param.12) | copy-start | bytes 3076
  64.4 14.0 %all-to-all-start = ((bf16[8,2,1024]{2,1,0:T(2,128)(2,1)}), bf16[8,2,1024]{2,1,0:T(2,128)(2,1)S(1)}, u32[]{:S(2)}, u32[]{:S(2)}) async-start(bf16[8,2,1024]{2,1,0:T(2,128)(2,1)} %reshape.289), calls=%async_computation | async-start | bytes 65536 | tf_op jit(solution)/shard_map/all_to_all | solution.py:20
  71.7 92.0 %all-reduce.2.cloned.1.call-start = ((), (), s32[]{:S(2)}) async-start(), calls=%async_computation.4 | async-start | bytes 327680 | tf_op jit(solution)/shard_map/psum | solution.py:24
  92.8 3.7 %copy-start.1 = (bf16[2048]{0:T(1024)(128)(2,1)S(1)}, bf16[2048]{0:T(1024)(128)(2,1)}, u32[]{:S(2)}) copy-start(bf16[2048]{0:T(1024)(128)(2,1)} %param.11) | copy-start | bytes 12292
  165.7 11.0 %all-to-all-start.1 = ((f32[1,2,8,2,8]{4,3,1,0,2:T(2,128)}), f32[1,2,8,2,8]{4,3,1,0,2:T(2,128)S(1)}, u32[]{:S(2)}, u32[]{:S(2)}) async-start(f32[1,2,8,2,8]{4,3,1,0,2:T(2,128)} %copy.44), calls=%async_computation.1 | async-start | bytes 32768 | tf_op jit(solution)/shard_map/all_to_all | solution.py:100
  176.6 9.9 %all-to-all-start.3 = ((f32[1,2,8,2,8]{4,3,1,0,2:T(2,128)}), f32[1,2,8,2,8]{4,3,1,0,2:T(2,128)S(1)}, u32[]{:S(2)}, u32[]{:S(2)}) async-start(f32[1,2,8,2,8]{4,3,1,0,2:T(2,128)} %copy.52), calls=%async_computation.3 | async-start | bytes 32768 | tf_op jit(solution)/shard_map/all_to_all | solution.py:103
  186.5 10.7 %all-to-all-start.2 = ((f32[1,2,8,2,8,128]{5,4,3,1,0,2:T(8,128)}), f32[1,2,8,2,8,128]{5,4,3,1,0,2:T(8,128)S(1)}, u32[]{:S(2)}, u32[]{:S(2)}) async-start(f32[1,2,8,2,8,128]{5,4,3,1,0,2:T(8,128)} %copy.49), calls=%async_computation.2 | async-start | bytes 262144 | tf_op jit(solution)/shard_map/all_to_all | solution.py:106
Sparse Core Ops, SparseCore 0:
  96.3 67.3 all-reduce.1
where the time goes:
time: 206 us; the launch traced here: 205 us
  waiting for transfers between devices  90.1 us (44%)
  other arithmetic  46.9 us (23%)
  local copies, waits for them, and re-layouts  31 us (15%)
  starting transfers between devices  18.4 us (9%)
  between operations  14.3 us (7%)
  matrix products  4.29 us (2%)
    psum x1, waiting for transfers between devices, shards(): lax.psum(jnp.dot(flat_rows, weights_all, preferred_element_type=jnp.float...  67.2 us
    unnamed x1, other arithmetic  45.3 us
    unnamed x18, local copies, waits for them, and re-layouts  19.2 us
    all_to_all x2, local copies, waits for them, and re-layouts, shards(): lax.all_to_all(hidden, 'ctx', split_axis=2, concat_axis=0, tiled=True)  8.11 us
    all_to_all x1, starting transfers between devices, shards(): lax.all_to_all(hidden, 'ctx', split_axis=2, concat_axis=0, tiled=True)  7.28 us
    all_to_all x1, waiting for transfers between devices, shards(): lax.all_to_all(closing_state[2].reshape(lead_shape + (HEAD_SIZE,)), 'ctx'...  7.2 us
    all_to_all x1, waiting for transfers between devices, shards(): lax.all_to_all(closing_state[1].reshape(lead_shape), 'ctx', split_axis=2,...  6.48 us
    all_to_all x1, waiting for transfers between devices, shards(): lax.all_to_all(hidden, 'ctx', split_axis=2, concat_axis=0, tiled=True)  4.69 us
  transfers between devices with their start and end apart: 5, of which 5 were waited for; matrix products, arithmetic and copies ran while one was open for 2% of the time, Pallas kernels for 0%

commit v1 on v0

--- a/solution.py
+++ b/solution.py
@@ -17,7 +17,9 @@
     query_group_width = q_width // k_width
     score_scale = HEAD_SIZE ** (-0.5)
     row_count = 2 * tok_dev
-    columns = lax.all_to_all(hidden, "ctx", split_axis=2, concat_axis=0, tiled=True)
+    pieces = jnp.split(hidden, lax.axis_size("ctx"), axis=2)
+    incoming = lax.all_to_all(jnp.stack(pieces), "ctx", 0, 0)
+    columns = jnp.concatenate(incoming, axis=0)
     flat_rows = columns.reshape(2 * resp_tokens, columns.shape[2])
     weights_all = jnp.concatenate((wq, wkv[0], wkv[1]), axis=1)
     bias_all = jnp.concatenate((bias_q, bias_kv[0], bias_kv[1])).astype(jnp.float32)

time: 206 us -> 146 us (0.71)
  other arithmetic: 46.9 us -> 2.88 us
  local copies, waits for them, and re-layouts: 31 us -> 16.2 us
    unnamed x1 -> x0, other arithmetic: 45.3 us -> none
    unnamed x18 -> x14, local copies, waits for them, and re-layouts: 19.2 us -> 9.29 us
    all_to_all x2 -> x0, local copies, waits for them, and re-layouts: 8.11 us -> none  [shards(): lax.all_to_all(hidden, 'ctx', split_axis=2, concat_axis=0, tiled=True)]
    all_to_all x1, waiting for transfers between devices: 4.69 us -> 1.46 us  [shards(): incoming = lax.all_to_all(jnp.stack(pieces), 'ctx', 0, 0)]
    psum x1, waiting for transfers between devices: 67.2 us -> 69.7 us  [shards(): lax.psum(jnp.dot(flat_rows, weights_all, preferred_element_type=jnp.float...]
  transfers between devices with their start and end apart: 5 -> 5, of which waited for: 5 -> 5; matrix products, arithmetic and copies ran while one was open for 2% -> 5% of each run, Pallas kernels for 0% -> 0%
where the time goes in v1:
time: 146 us
  waiting for transfers between devices  89.4 us (61%)
  starting transfers between devices  18.4 us (13%)
  local copies, waits for them, and re-layouts  16.2 us (11%)
  between operations  14.2 us (10%)
  matrix products  4.29 us (3%)
  other arithmetic  2.88 us (2%)
    psum x1, waiting for transfers between devices, shards(): lax.psum(jnp.dot(flat_rows, weights_all, preferred_element_type=jnp.float...  69.7 us
    unnamed x14, local copies, waits for them, and re-layouts  9.29 us
    all_to_all x1, starting transfers between devices, shards(): incoming = lax.all_to_all(jnp.stack(pieces), 'ctx', 0, 0)  7.28 us
    all_to_all x1, waiting for transfers between devices, shards(): lax.all_to_all(closing_state[2].reshape(lead_shape + (HEAD_SIZE,)), 'ctx'...  7.2 us
    all_to_all x1, waiting for transfers between devices, shards(): lax.all_to_all(closing_state[1].reshape(lead_shape), 'ctx', split_axis=2,...  6.48 us
    all_to_all x1, waiting for transfers between devices, shards(): lax.all_to_all(closing_state[0].reshape(lead_shape), 'ctx', split_axis=2,...  4.54 us
    all_to_all x1, starting transfers between devices, shards(): lax.all_to_all(closing_state[0].reshape(lead_shape), 'ctx', split_axis=2,...  4.4 us
    all_to_all x1, starting transfers between devices, shards(): lax.all_to_all(closing_state[2].reshape(lead_shape + (HEAD_SIZE,)), 'ctx'...  3.37 us
  transfers between devices with their start and end apart: 5, of which 5 were waited for; matrix products, arithmetic and copies ran while one was open for 5% of the time, Pallas kernels for 0%

profile of v1, /device:TPU:0, one launch (start us, length us, event | category | flops | bytes accessed | tf_op | source)
XLA Modules:
  0.0 145.5 jit_solution(17197644539874577633)
XLA Ops:
  6.5 1.3 constant_dynamic-update-slice_fusion.7
  7.8 1.3 constant_dynamic-update-slice_fusion.6
  9.1 1.3 constant_dynamic-update-slice_fusion.5
  10.4 1.3 constant_dynamic-update-slice_fusion.4
  11.7 1.3 constant_dynamic-update-slice_fusion.3
  12.9 1.3 constant_dynamic-update-slice_fusion.2
  14.2 1.3 constant_dynamic-update-slice_fusion.1
  15.5 1.3 constant_dynamic-update-slice_fusion
  16.8 7.3 %all-to-all-start = ((bf16[8,1,2,1024]{3,2,1,0:T(2,128)(2,1)}), bf16[8,1,2,1024]{3,2,1,0:T(2,128)(2,1)S(1)}, u32[]{:S(2)}, u32[]{:S(2)}) async-start(bf16[8,1,2,1024]{3,2,1,0:T(2,128)(2,1)} %constant_dynamic-update-slice_fusion), calls=%async_computation | async-start | bytes 65536 | tf_op jit(solution)/shard_map/all_to_all | solution.py:21
  24.1 1.3 slice_bitcast_fusion.1
  25.4 0.7 broadcast_compare_fusion
  26.1 0.7 compare_and_fusion
  27.4 1.1 fusion.42
  28.5 0.8 slice_reduce_fusion.1
  29.3 1.5 %all-to-all-done = bf16[8,1,2,1024]{3,2,1,0:T(2,128)(2,1)S(1)} async-done(((bf16[8,1,2,1024]{3,2,1,0:T(2,128)(2,1)}), bf16[8,1,2,1024]{3,2,1,0:T(2,128)(2,1)S(1)}, u32[]{:S(2)}, u32[]{:S(2)}) %all-to-all-start) | async-done | bytes 32800 | tf_op jit(solution)/shard_map/all_to_all | solution.py:21
  30.8 3.3 %fusion = f32[16,2560]{1,0:T(8,128)} fusion(bf16[16,1024]{1,0:T(8,128)(2,1)S(1)} %reshape_reshape.3, bf16[1024,256]{1,0:T(8,128)(2,1)S(1)} %get-tuple-element.26, bf16[1024,256]{1,0:T(8,128)(2,1)S(1)} %get-tuple-element.25, bf16[1024,2048]{1,0:T(8,128)(2,1)} %param.9), kind=kOutput, calls=%fused_computation | convolution fusion | flops 99614720 | bytes 5439488 | tf_op jit(solution)/shard_map/dot_general | solution.py:26
  34.5 69.7 %all-reduce.2.cloned.1.call-done = f32[16,2560]{1,0:T(8,128)} async-done(((f32[16,2560]{1,0:T(8,128)}), f32[16,2560]{1,0:T(8,128)}) %all-reduce.2.cloned.1.call-update) | async-done | bytes 163856 | tf_op jit(solution)/shard_map/psum | solution.py:26
  104.2 0.9 add_convert_fusion
  106.2 4.4 %all-to-all-start.1 = ((f32[1,2,8,2,8]{4,3,1,0,2:T(2,128)}), f32[1,2,8,2,8]{4,3,1,0,2:T(2,128)S(1)}, u32[]{:S(2)}, u32[]{:S(2)}) async-start(f32[1,2,8,2,8]{4,3,1,0,2:T(2,128)} %copy.38), calls=%async_computation.1 | async-start | bytes 32768 | tf_op jit(solution)/shard_map/all_to_all | solution.py:102
  112.6 4.5 %all-to-all-done.1 = f32[1,2,8,2,8]{4,3,1,0,2:T(2,128)S(1)} async-done(((f32[1,2,8,2,8]{4,3,1,0,2:T(2,128)}), f32[1,2,8,2,8]{4,3,1,0,2:T(2,128)S(1)}, u32[]{:S(2)}, u32[]{:S(2)}) %all-to-all-start.1) | async-done | bytes 1056 | tf_op jit(solution)/shard_map/all_to_all | solution.py:102
  117.2 3.3 %all-to-all-start.3 = ((f32[1,2,8,2,8]{4,3,1,0,2:T(2,128)}), f32[1,2,8,2,8]{4,3,1,0,2:T(2,128)S(1)}, u32[]{:S(2)}, u32[]{:S(2)}) async-start(f32[1,2,8,2,8]{4,3,1,0,2:T(2,128)} %copy.46), calls=%async_computation.3 | async-start | bytes 32768 | tf_op jit(solution)/shard_map/all_to_all | solution.py:105
  120.5 6.5 %all-to-all-done.3 = f32[1,2,8,2,8]{4,3,1,0,2:T(2,128)S(1)} async-done(((f32[1,2,8,2,8]{4,3,1,0,2:T(2,128)}), f32[1,2,8,2,8]{4,3,1,0,2:T(2,128)S(1)}, u32[]{:S(2)}, u32[]{:S(2)}) %all-to-all-start.3) | async-done | bytes 1056 | tf_op jit(solution)/shard_map/all_to_all | solution.py:105
  127.0 3.4 %all-to-all-start.2 = ((f32[1,2,8,2,8,128]{5,4,3,1,0,2:T(8,128)}), f32[1,2,8,2,8,128]{5,4,3,1,0,2:T(8,128)S(1)}, u32[]{:S(2)}, u32[]{:S(2)}) async-start(f32[1,2,8,2,8,128]{5,4,3,1,0,2:T(8,128)} %copy.43), calls=%async_computation.2 | async-start | bytes 262144 | tf_op jit(solution)/shard_map/all_to_all | solution.py:108
  130.5 7.2 %all-to-all-done.2 = f32[1,2,8,2,8,128]{5,4,3,1,0,2:T(8,128)S(1)} async-done(((f32[1,2,8,2,8,128]{5,4,3,1,0,2:T(8,128)}), f32[1,2,8,2,8,128]{5,4,3,1,0,2:T(8,128)S(1)}, u32[]{:S(2)}, u32[]{:S(2)}) %all-to-all-start.2) | async-done | bytes 131104 | tf_op jit(solution)/shard_map/all_to_all | solution.py:108
  (35 shorter events, 4.4 us)
Async XLA Ops:
  16.8 14.0 %all-to-all-start = ((bf16[8,1,2,1024]{3,2,1,0:T(2,128)(2,1)}), bf16[8,1,2,1024]{3,2,1,0:T(2,128)(2,1)S(1)}, u32[]{:S(2)}, u32[]{:S(2)}) async-start(bf16[8,1,2,1024]{3,2,1,0:T(2,128)(2,1)} %constant_dynamic-update-slice_fusion), calls=%async_computation | async-start | bytes 65536 | tf_op jit(solution)/shard_map/all_to_all | solution.py:21
  24.1 80.2 %all-reduce.2.cloned.1.call-start = ((), (), s32[]{:S(2)}) async-start(), calls=%async_computation.4 | async-start | bytes 327680 | tf_op jit(solution)/shard_map/psum | solution.py:26
  30.8 3.7 %copy-start = (bf16[2048]{0:T(1024)(128)(2,1)S(1)}, bf16[2048]{0:T(1024)(128)(2,1)}, u32[]{:S(2)}) copy-start(bf16[2048]{0:T(1024)(128)(2,1)} %param.11) | copy-start | bytes 12292
  106.2 11.0 %all-to-all-start.1 = ((f32[1,2,8,2,8]{4,3,1,0,2:T(2,128)}), f32[1,2,8,2,8]{4,3,1,0,2:T(2,128)S(1)}, u32[]{:S(2)}, u32[]{:S(2)}) async-start(f32[1,2,8,2,8]{4,3,1,0,2:T(2,128)} %copy.38), calls=%async_computation.1 | async-start | bytes 32768 | tf_op jit(solution)/shard_map/all_to_all | solution.py:102
  117.2 9.9 %all-to-all-start.3 = ((f32[1,2,8,2,8]{4,3,1,0,2:T(2,128)}), f32[1,2,8,2,8]{4,3,1,0,2:T(2,128)S(1)}, u32[]{:S(2)}, u32[]{:S(2)}) async-start(f32[1,2,8,2,8]{4,3,1,0,2:T(2,128)} %copy.46), calls=%async_computation.3 | async-start | bytes 32768 | tf_op jit(solution)/shard_map/all_to_all | solution.py:105
  127.0 10.7 %all-to-all-start.2 = ((f32[1,2,8,2,8,128]{5,4,3,1,0,2:T(8,128)}), f32[1,2,8,2,8,128]{5,4,3,1,0,2:T(8,128)S(1)}, u32[]{:S(2)}, u32[]{:S(2)}) async-start(f32[1,2,8,2,8,128]{5,4,3,1,0,2:T(8,128)} %copy.43), calls=%async_computation.2 | async-start | bytes 262144 | tf_op jit(solution)/shard_map/all_to_all | solution.py:108
Sparse Core Ops, SparseCore 0:
  34.3 69.9 all-reduce.1
